TPU v7x, 512 devices: a whole 4x8x8 slice. The times are simulated.
512 devices in a mesh: row: 16 (over z, core), col: 32 (over x, y).
Axes of the slice: x: 4, y: 8, z: 8, core: 2. Of those that a mesh axis runs over, the one named last changes fastest.
Arguments:
- u_front: bfloat16 [2, 2048, 25, 2048], P(None, 'col', None, 'row'), may hold values from -0.02734375 to 0.02734375
- inverse_blocks: bfloat16 [2, 2048, 1, 2048], P(None, 'col', None, 'row')
- rhs_window: float32 [32, 2, 2048], P(None, None, 'col'), may hold values from -6 to 6
- pivot_inverse: float32 [2, 2048], P(None, 'col'), may hold values from 0.25 to 4
- below_solution: bfloat16 [32, 23, 2048], P(None, None, 'row'), may hold values from -6 to 6
- u_child: bfloat16 [4096, 16, 2048], P('col', None, 'row'), may hold values from -0.03125 to 0.03125
- rhs_child: float32 [32, 4096], P(None, 'col'), may hold values from -6 to 6
- child_map: int32 [2, 256], replicated, may hold values from 0 to 399, as said below
- child_counts: int32 [2], replicated, may hold values from 128 to 256, as said below
Outputs:
- x_window: float32 [32, 2, 2048], P(None, None, 'row')
- child_out: float32 [32, 4096], P(None, 'col')
Inputs may be any that keep to these rules, and one draw needn't show every extreme that they name: Slot s of a child lies on row index s % 16 of the child's rows, and the block it names lies on row index (s % 16 + s // 16) % 16 of the front's rows, that is child_map[h, s] % 16 equals that number; one child names each block at most once; both ends of the range are named. `child_counts`: one of the two children uses all 256 slots.
All inputs are finite; a program needn't handle non-finite values.
Results may differ from a plain program's by a relative error of at most 0.003.
Values may be sent and summed in bfloat16 or wider, within the bound.
A program may use at most 64 MiB of HBM per device.

v0:
```python
import jax
import jax.numpy as jnp
from jax import lax
from jax.sharding import PartitionSpec as P


def local(
    u_front,
    inverse_blocks,
    rhs_window,
    pivot_inverse,
    below_solution,
    u_child,
    rhs_child,
    child_map,
    child_counts,
):
    panel_count = u_front.shape[0]
    front_blocks = u_front.shape[2]
    block_rows = u_front.shape[3]
    panel_blocks = inverse_blocks.shape[2]
    window_blocks = panel_count * panel_blocks
    rhs_count = rhs_window.shape[0]
    scaled = rhs_window * pivot_inverse[None]
    solved = [None] * panel_count
    solved_rows = jnp.concatenate(
        [jnp.zeros((rhs_count, window_blocks, block_rows), jnp.bfloat16), below_solution], axis=1
    )
    for panel_index in reversed(range(panel_count)):
        partial_value = jnp.einsum(
            "wqb,nqb->nw", u_front[panel_index], solved_rows, preferred_element_type=jnp.float32
        )
        summed = lax.psum(partial_value, "row")
        reduced = (scaled[:, panel_index] - summed).astype(jnp.bfloat16)
        partial_share = jnp.einsum(
            "nw,wpb->npb", reduced, inverse_blocks[panel_index], preferred_element_type=jnp.float32
        )
        result = lax.psum(partial_share, "col")
        solved[panel_index] = result
        lower_edge = panel_index * panel_blocks
        solved_rows = lax.dynamic_update_slice_in_dim(
            solved_rows, result.astype(jnp.bfloat16), lower_edge, 1
        )
    x_window = jnp.concatenate(solved, axis=1)
    row_count = lax.axis_size("row")
    my_row = lax.axis_index("row")
    half_width = lax.axis_size("col") // 2
    which_child = lax.axis_index("col") // half_width
    slot_depth = u_child.shape[1]
    child_slots = child_map[which_child]
    local_slots = jnp.arange(slot_depth, dtype=jnp.int32) * row_count + my_row
    wanted = child_slots[local_slots]
    live_mask = (local_slots < child_counts[which_child]).astype(jnp.bfloat16)
    section = lax.all_gather(solved_rows, "row", axis=1, tiled=True)
    length = section.shape[1]
    gathered_index = jnp.arange(length, dtype=jnp.int32)
    global_block = gathered_index % front_blocks * row_count + gathered_index // front_blocks
    selector = (wanted[:, None] == global_block[None, :]).astype(jnp.bfloat16)
    incoming = jnp.einsum(
        "sq,nqb->nsb", selector, section, preferred_element_type=jnp.float32
    ).astype(jnp.bfloat16)
    masked = incoming * live_mask[None, :, None]
    child_part = jnp.einsum("psb,nsb->np", u_child, masked, preferred_element_type=jnp.float32)
    child_total = lax.psum(child_part, "row")
    child_out = rhs_child - child_total
    return (x_window, child_out)


def solution(mesh):
    return jax.shard_map(
        local,
        mesh=mesh,
        in_specs=(
            P(None, "col", None, "row"),
            P(None, "col", None, "row"),
            P(None, None, "col"),
            P(None, "col"),
            P(None, None, "row"),
            P("col", None, "row"),
            P(None, "col"),
            P(),
            P(),
        ),
        out_specs=(P(None, None, "row"), P(None, "col")),
        check_vma=False,
    )
```

profile of v0, /device:TPU:2, one launch (start us, length us, event | category | flops | bytes accessed | tf_op | source)
XLA Modules:
  0.0 485.7 jit_solution(11730641307680731013)
XLA Ops:
  7.2 0.0 copy-start
  7.2 0.0 all-gather.2.cloned.1.call-start
  7.2 1.4 convolution_bitcast_fusion.3
  8.6 54.0 %psum.35 = f32[32,64]{1,0:T(8,128)S(1)} all-reduce(f32[32,64]{1,0:T(8,128)S(1)} %convolution_bitcast_fusion.3), channel_id=1, replica_groups=mesh['row'=16,'col'=32] {'row'}, use_global_device_ids=true, to_apply=%region_0.0 | all-reduce | flops 2048 | bytes 16384 | tf_op jit(solution)/shard_map/psum | solution.py:33
  62.6 0.8 copy_multiply_fusion
  63.4 0.8 convolution_bitcast_fusion.2
  64.3 131.2 %psum.36 = f32[32,1,128]{2,0,1:T(8,128)S(1)} all-reduce(f32[32,1,128]{2,0,1:T(8,128)S(1)} %convolution_bitcast_fusion.2), channel_id=1, replica_groups=mesh['row'=16,'col'=32] {'col'}, use_global_device_ids=true, to_apply=%region_1.0 | all-reduce | flops 4096 | bytes 32768 | tf_op jit(solution)/shard_map/psum | solution.py:38
  195.5 0.9 concatenate.6
  196.4 1.2 convolution_bitcast_fusion.4
  197.7 45.7 %psum.37 = f32[32,64]{1,0:T(8,128)S(1)} all-reduce(f32[32,64]{1,0:T(8,128)S(1)} %convolution_bitcast_fusion.4), channel_id=1, replica_groups=mesh['row'=16,'col'=32] {'row'}, use_global_device_ids=true, to_apply=%region_2.0 | all-reduce | flops 2048 | bytes 16384 | tf_op jit(solution)/shard_map/psum | solution.py:33
  243.4 0.8 convolution_bitcast_fusion.1
  244.2 137.7 %psum.38 = f32[32,1,128]{2,0,1:T(8,128)S(1)} all-reduce(f32[32,1,128]{2,0,1:T(8,128)S(1)} %convolution_bitcast_fusion.1), channel_id=1, replica_groups=mesh['row'=16,'col'=32] {'col'}, use_global_device_ids=true, to_apply=%region_3.0 | all-reduce | flops 4096 | bytes 32768 | tf_op jit(solution)/shard_map/psum | solution.py:38
  381.9 0.7 copy-done.1
  382.6 0.0 all-gather.2.cloned.1.call-update
  382.6 0.6 copy.19
  383.3 1.2 dynamic_slice.7
  384.5 0.7 constant_dynamic-slice_fusion
  385.2 0.7 gather_fusion
  385.9 0.7 compare_convert_fusion
  386.5 41.5 %all-gather.2.cloned.1.call-done = bf16[32,400,128]{2,0,1:T(8,128)(2,1)} async-done(((bf16[32,25,128]{2,0,1:T(8,128)(2,1)}), bf16[32,400,128]{2,0,1:T(8,128)(2,1)}) %all-gather.2.cloned.1.call-update) | async-done | bytes 3276816 | tf_op jit(solution)/shard_map/all_gather | solution.py:54
  428.1 2.9 fusion.8
  431.0 0.3 convolution_bitcast_fusion
  431.2 47.0 %psum.39 = f32[32,128]{1,0:T(8,128)S(1)} all-reduce(f32[32,128]{1,0:T(8,128)S(1)} %convolution_bitcast_fusion), channel_id=1, replica_groups=mesh['row'=16,'col'=32] {'row'}, use_global_device_ids=true, to_apply=%region_4.5 | all-reduce | flops 4096 | bytes 32768 | tf_op jit(solution)/shard_map/psum | solution.py:64
  478.3 0.6 sub.23
  (10 shorter events, 0.1 us)
Async XLA Ops:
  7.2 423.8 %copy-start = (bf16[128,16,128]{2,1,0:T(8,128)(2,1)S(1)}, bf16[128,16,128]{2,1,0:T(8,128)(2,1)}, u32[]{:S(2)}) copy-start(bf16[128,16,128]{2,1,0:T(8,128)(2,1)} %param.14) | copy-start | bytes 1572868
  7.2 420.9 %all-gather.2.cloned.1.call-start = ((), (), s32[]{:S(2)}) async-start(), calls=%async_computation | async-start | bytes 3481600 | tf_op jit(solution)/shard_map/all_gather | solution.py:54
  196.4 281.9 %copy-start.2 = (f32[32,128]{1,0:T(8,128)S(1)}, f32[32,128]{1,0:T(8,128)}, u32[]{:S(2)}) copy-start(f32[32,128]{1,0:T(8,128)} %param.15) | copy-start | bytes 49156
  381.9 0.7 copy-start.1
Sparse Core Ops, SparseCore 0:
  382.7 45.3 all-gather.1
where the time goes:
time: 486 us
  blocking collectives  416 us (86%)
  waiting for transfers between devices  41.5 us (9%)
  between operations  14.1 us (3%)
  matrix products  7.46 us (2%)
  local copies, waits for them, and re-layouts  4.87 us (1%)
    psum x2, blocking collectives, local(): result = lax.psum(partial_share, 'col')  269 us
    psum x2, blocking collectives, local(): summed = lax.psum(partial_value, 'row')  99.7 us
    psum x1, blocking collectives, local(): child_total = lax.psum(child_part, 'row')  47 us
    all_gather x1, waiting for transfers between devices, local(): section = lax.all_gather(solved_rows, 'row', axis=1, tiled=True)  41.5 us
  transfers between devices with their start and end apart: 1, of which 1 were waited for; matrix products, arithmetic and copies ran while one was open for 1% of the time, Pallas kernels for 0%

commit v1 on v0

--- a/solution.py
+++ b/solution.py
@@ -15,6 +15,15 @@
     child_map,
     child_counts,
 ):
+
+    def get_page(xin):
+        return jnp.concatenate(
+            lax.all_to_all(
+                jnp.stack(tuple((xin for _ in range(lax.axis_size("row"))))), "row", 0, 0
+            ),
+            axis=1,
+        )
+
     panel_count = u_front.shape[0]
     front_blocks = u_front.shape[2]
     block_rows = u_front.shape[3]
@@ -51,7 +60,7 @@
     local_slots = jnp.arange(slot_depth, dtype=jnp.int32) * row_count + my_row
     wanted = child_slots[local_slots]
     live_mask = (local_slots < child_counts[which_child]).astype(jnp.bfloat16)
-    section = lax.all_gather(solved_rows, "row", axis=1, tiled=True)
+    section = get_page(solved_rows)
     length = section.shape[1]
     gathered_index = jnp.arange(length, dtype=jnp.int32)
     global_block = gathered_index % front_blocks * row_count + gathered_index // front_blocks

time: 486 us -> 518 us (1.066)
  the two profiles are of different devices: /device:TPU:2 before, /device:TPU:1 now
where the time goes in v1:
time: 518 us
  blocking collectives  395 us (76%)
  waiting for transfers between devices  71.4 us (14%)
  starting transfers between devices  35.2 us (7%)
  matrix products  7.45 us (1%)
  local copies, waits for them, and re-layouts  5.76 us (1%)
    psum x2, blocking collectives, local(): result = lax.psum(partial_share, 'col')  226 us
    psum x2, blocking collectives, local(): summed = lax.psum(partial_value, 'row')  125 us
    all_to_all x1, waiting for transfers between devices, get_page(): lax.all_to_all(jnp.stack(tuple((xin for _ in range(lax.axis_size('row')))...  71.4 us
    psum x1, blocking collectives, local(): child_total = lax.psum(child_part, 'row')  43.5 us
    all_to_all x1, starting transfers between devices, get_page(): lax.all_to_all(jnp.stack(tuple((xin for _ in range(lax.axis_size('row')))...  35.2 us
  transfers between devices with their start and end apart: 1, of which 1 were waited for; matrix products, arithmetic and copies ran while one was open for 0% of the time, Pallas kernels for 0%

profile of v1, /device:TPU:1, one launch (start us, length us, event | category | flops | bytes accessed | tf_op | source)
XLA Modules:
  0.0 517.5 jit_solution(8953386282456057238)
XLA Ops:
  0.6 0.0 copy-start
  0.6 0.7 broadcast.111
  1.4 0.8 broadcast_multiply_fusion
  2.2 1.3 convolution_bitcast_fusion.3
  3.5 52.0 %psum.35 = f32[32,64]{1,0:T(8,128)S(1)} all-reduce(f32[32,64]{1,0:T(8,128)S(1)} %convolution_bitcast_fusion.3), channel_id=1, replica_groups=mesh['row'=16,'col'=32] {'row'}, use_global_device_ids=true, to_apply=%region_0.0 | all-reduce | flops 2048 | bytes 16384 | tf_op jit(solution)/shard_map/psum | solution.py:42
  55.5 0.8 convolution_bitcast_fusion.2
  56.4 115.7 %psum.36 = f32[32,1,128]{2,0,1:T(8,128)S(1)} all-reduce(f32[32,1,128]{2,0,1:T(8,128)S(1)} %convolution_bitcast_fusion.2), channel_id=1, replica_groups=mesh['row'=16,'col'=32] {'col'}, use_global_device_ids=true, to_apply=%region_1.0 | all-reduce | flops 4096 | bytes 32768 | tf_op jit(solution)/shard_map/psum | solution.py:47
  172.1 0.9 concatenate.6
  173.0 1.2 convolution_bitcast_fusion.4
  174.3 73.3 %psum.37 = f32[32,64]{1,0:T(8,128)S(1)} all-reduce(f32[32,64]{1,0:T(8,128)S(1)} %convolution_bitcast_fusion.4), channel_id=1, replica_groups=mesh['row'=16,'col'=32] {'row'}, use_global_device_ids=true, to_apply=%region_2.0 | all-reduce | flops 2048 | bytes 16384 | tf_op jit(solution)/shard_map/psum | solution.py:42
  247.6 0.8 convolution_bitcast_fusion.1
  248.4 110.3 %psum.38 = f32[32,1,128]{2,0,1:T(8,128)S(1)} all-reduce(f32[32,1,128]{2,0,1:T(8,128)S(1)} %convolution_bitcast_fusion.1), channel_id=1, replica_groups=mesh['row'=16,'col'=32] {'col'}, use_global_device_ids=true, to_apply=%region_3.0 | all-reduce | flops 4096 | bytes 32768 | tf_op jit(solution)/shard_map/psum | solution.py:47
  358.8 2.1 stack.2
  360.9 35.2 %all-to-all-start = ((bf16[16,32,25,128]{3,1,2,0:T(8,128)(2,1)}), bf16[16,32,25,128]{3,1,2,0:T(8,128)(2,1)}, u32[]{:S(2)}, u32[]{:S(2)}) async-start(bf16[16,32,25,128]{3,1,2,0:T(8,128)(2,1)} %stack.2), calls=%async_computation | async-start | bytes 6553600 | tf_op jit(solution)/shard_map/all_to_all | solution.py:21
  396.1 0.6 copy.15
  396.8 0.6 dynamic_slice.7
  397.4 0.7 gather_fusion
  398.1 0.7 compare_convert_fusion
  398.7 71.4 %all-to-all-done = bf16[16,32,25,128]{3,1,2,0:T(8,128)(2,1)} async-done(((bf16[16,32,25,128]{3,1,2,0:T(8,128)(2,1)}), bf16[16,32,25,128]{3,1,2,0:T(8,128)(2,1)}, u32[]{:S(2)}, u32[]{:S(2)}) %all-to-all-start) | async-done | bytes 3276832 | tf_op jit(solution)/shard_map/all_to_all | solution.py:21
  470.1 2.9 fusion
  473.0 0.3 convolution_bitcast_fusion
  473.4 43.5 %psum.39 = f32[32,128]{1,0:T(8,128)S(1)} all-reduce(f32[32,128]{1,0:T(8,128)S(1)} %convolution_bitcast_fusion), channel_id=1, replica_groups=mesh['row'=16,'col'=32] {'row'}, use_global_device_ids=true, to_apply=%region_4.5 | all-reduce | flops 4096 | bytes 32768 | tf_op jit(solution)/shard_map/psum | solution.py:73
  516.9 0.0 copy-done.1
  516.9 0.6 sub.23
  (14 shorter events, 0.1 us)
Async XLA Ops:
  0.6 472.4 %copy-start = (bf16[128,16,128]{2,1,0:T(8,128)(2,1)S(1)}, bf16[128,16,128]{2,1,0:T(8,128)(2,1)}, u32[]{:S(2)}) copy-start(bf16[128,16,128]{2,1,0:T(8,128)(2,1)} %param.14) | copy-start | bytes 1572868
  360.9 35.9 %copy-start.3 = (s32[2]{0:T(128)S(1)}, s32[2]{0:T(128)}, u32[]{:S(2)}) copy-start(s32[2]{0:T(128)} %param.17) | copy-start | bytes 28
  360.9 36.5 %copy-start.2 = (s32[2,256]{1,0:T(2,128)S(1)}, s32[2,256]{1,0:T(2,128)}, u32[]{:S(2)}) copy-start(s32[2,256]{1,0:T(2,128)} %param.16) | copy-start | bytes 6148
  360.9 109.2 %all-to-all-start = ((bf16[16,32,25,128]{3,1,2,0:T(8,128)(2,1)}), bf16[16,32,25,128]{3,1,2,0:T(8,128)(2,1)}, u32[]{:S(2)}, u32[]{:S(2)}) async-start(bf16[16,32,25,128]{3,1,2,0:T(8,128)(2,1)} %stack.2), calls=%async_computation | async-start | bytes 6553600 | tf_op jit(solution)/shard_map/all_to_all | solution.py:21
  396.1 120.8 %copy-start.1 = (f32[32,128]{1,0:T(8,128)S(1)}, f32[32,128]{1,0:T(8,128)}, u32[]{:S(2)}) copy-start(f32[32,128]{1,0:T(8,128)} %param.15) | copy-start | bytes 49156

commit v2 on v0

--- a/solution.py
+++ b/solution.py
@@ -35,7 +35,8 @@
         partial_share = jnp.einsum(
             "nw,wpb->npb", reduced, inverse_blocks[panel_index], preferred_element_type=jnp.float32
         )
-        result = lax.psum(partial_share, "col")
+        parts = lax.all_gather(partial_share, "col")
+        result = jnp.sum(parts, axis=0)
         solved[panel_index] = result
         lower_edge = panel_index * panel_blocks
         solved_rows = lax.dynamic_update_slice_in_dim(

time: 486 us -> 309 us (0.64)
  blocking collectives: 416 us -> 244 us
    psum x2 -> x0, blocking collectives: 269 us -> none  [local(): result = lax.psum(partial_share, 'col')]
    all_gather x0 -> x2, blocking collectives: none -> 97.2 us  [local(): parts = lax.all_gather(partial_share, 'col')]
where the time goes in v2:
time: 309 us; the launch traced here: 308 us
  blocking collectives  244 us (79%)
  waiting for transfers between devices  36.8 us (12%)
  between operations  14.1 us (5%)
  matrix products  7.46 us (2%)
  local copies, waits for them, and re-layouts  3.53 us (1%)
    psum x2, blocking collectives, local(): summed = lax.psum(partial_value, 'row')  99.7 us
    all_gather x2, blocking collectives, local(): parts = lax.all_gather(partial_share, 'col')  97.2 us
    psum x1, blocking collectives, local(): child_total = lax.psum(child_part, 'row')  47 us
    all_gather x1, waiting for transfers between devices, local(): section = lax.all_gather(solved_rows, 'row', axis=1, tiled=True)  36.7 us
  transfers between devices with their start and end apart: 1, of which 1 were waited for; matrix products, arithmetic and copies ran while one was open for 1% of the time, Pallas kernels for 0%

profile of v2, /device:TPU:2, one launch (start us, length us, event | category | flops | bytes accessed | tf_op | source)
XLA Modules:
  0.0 308.1 jit_solution(13128495248027180070)
XLA Ops:
  7.2 0.0 copy-start
  7.2 0.0 copy-start.4
  7.2 0.0 all-gather.4.cloned.1.call-start
  7.2 1.4 convolution_bitcast_fusion.1
  8.6 54.0 %psum.21 = f32[32,64]{1,0:T(8,128)S(1)} all-reduce(f32[32,64]{1,0:T(8,128)S(1)} %convolution_bitcast_fusion.1), channel_id=1, replica_groups=mesh['row'=16,'col'=32] {'row'}, use_global_device_ids=true, to_apply=%region_0.0 | all-reduce | flops 2048 | bytes 16384 | tf_op jit(solution)/shard_map/psum | solution.py:33
  62.7 0.8 copy_multiply_fusion
  63.4 0.8 fusion.25
  64.3 49.6 %all-gather = f32[1024,128]{1,0:T(8,128)S(1)} all-gather(f32[32,128]{1,0:T(8,128)S(1)} %fusion.25), channel_id=2, replica_groups=mesh['row'=16,'col'=32] {'col'}, dimensions={0}, use_global_device_ids=true | all-gather | bytes 540672 | tf_op jit(solution)/shard_map/all_gather | solution.py:38
  113.9 0.9 concatenate.6
  114.9 1.2 convolution_bitcast_fusion.2
  116.2 45.7 %psum.22 = f32[32,64]{1,0:T(8,128)S(1)} all-reduce(f32[32,64]{1,0:T(8,128)S(1)} %convolution_bitcast_fusion.2), channel_id=1, replica_groups=mesh['row'=16,'col'=32] {'row'}, use_global_device_ids=true, to_apply=%region_2.0 | all-reduce | flops 2048 | bytes 16384 | tf_op jit(solution)/shard_map/psum | solution.py:33
  161.9 0.8 fusion.23
  162.7 47.6 %all-gather.1 = f32[1024,128]{1,0:T(8,128)S(1)} all-gather(f32[32,128]{1,0:T(8,128)S(1)} %fusion.23), channel_id=3, replica_groups=mesh['row'=16,'col'=32] {'col'}, dimensions={0}, use_global_device_ids=true | all-gather | bytes 540672 | tf_op jit(solution)/shard_map/all_gather | solution.py:38
  210.3 0.7 copy-done.1
  211.0 0.0 all-gather.4.cloned.1.call-update
  211.1 0.6 copy.21
  211.7 0.6 dynamic_slice.7
  212.3 0.7 gather_fusion
  213.0 0.7 compare_convert_fusion
  213.7 36.7 %all-gather.4.cloned.1.call-done = bf16[32,400,128]{2,0,1:T(8,128)(2,1)} async-done(((bf16[32,25,128]{2,0,1:T(8,128)(2,1)}), bf16[32,400,128]{2,0,1:T(8,128)(2,1)}) %all-gather.4.cloned.1.call-update) | async-done | bytes 3276816 | tf_op jit(solution)/shard_map/all_gather | solution.py:55
  250.4 2.9 fusion.8
  253.3 0.3 convolution_bitcast_fusion
  253.6 47.0 %psum.23 = f32[32,128]{1,0:T(8,128)S(1)} all-reduce(f32[32,128]{1,0:T(8,128)S(1)} %convolution_bitcast_fusion), channel_id=1, replica_groups=mesh['row'=16,'col'=32] {'row'}, use_global_device_ids=true, to_apply=%region_4.5 | all-reduce | flops 4096 | bytes 32768 | tf_op jit(solution)/shard_map/psum | solution.py:65
  300.6 0.6 sub.23
  (16 shorter events, 0.2 us)
Async XLA Ops:
  7.2 246.1 %copy-start = (bf16[128,16,128]{2,1,0:T(8,128)(2,1)S(1)}, bf16[128,16,128]{2,1,0:T(8,128)(2,1)}, u32[]{:S(2)}) copy-start(bf16[128,16,128]{2,1,0:T(8,128)(2,1)} %param.14) | copy-start | bytes 1572868
  7.2 204.5 %copy-start.4 = (s32[2]{0:T(128)S(1)}, s32[2]{0:T(128)}, u32[]{:S(2)}) copy-start(s32[2]{0:T(128)} %param.17) | copy-start | bytes 28
  7.2 205.1 %copy-start.3 = (s32[2,256]{1,0:T(2,128)S(1)}, s32[2,256]{1,0:T(2,128)}, u32[]{:S(2)}) copy-start(s32[2,256]{1,0:T(2,128)} %param.16) | copy-start | bytes 6148
  7.2 243.2 %all-gather.4.cloned.1.call-start = ((), (), s32[]{:S(2)}) async-start(), calls=%async_computation | async-start | bytes 3481600 | tf_op jit(solution)/shard_map/all_gather | solution.py:55
  210.3 90.4 %copy-start.2 = (f32[32,128]{1,0:T(8,128)S(1)}, f32[32,128]{1,0:T(8,128)}, u32[]{:S(2)}) copy-start(f32[32,128]{1,0:T(8,128)} %param.15) | copy-start | bytes 49156
  210.3 0.7 copy-start.1
Sparse Core Ops, SparseCore 0:
  211.2 39.2 all-gather.3
